TPU v7x, 512 devices: a whole 4x8x8 slice. The times are simulated.
512 devices in a mesh: sec: 4 (over y_hi), gx: 16 (over z, core), gy: 8 (over y_lo, x).
Axes of the slice: x: 4, y: 8 (y_hi: 4, y_lo: 2; y = y_hi * 2 + y_lo), z: 8, core: 2. Of those that a mesh axis runs over, the one named last changes fastest.
Arguments:
- composition_matrix: float32 [22, 128, 128, 512], P(None, 'gx', 'gy', 'sec'), may hold values from 0 to 1
- local_mixing_coefficient: float32 [128, 128, 512], P('gx', 'gy', 'sec'), may hold values from 0.3 to 3
- thermal_field: float32 [128, 128, 512], P('gx', 'gy', 'sec'), may hold values from 0.5 to 2
- component_mixing_weight: float32 [22], replicated, may hold values from 0.05 to 1
- kinetics_jacobian: float32 [22, 22], replicated, may hold values from -1.25 to 1.25
- mixture_classes: int32 [128, 128, 512], P('gx', 'gy', 'sec'), may hold values from 0 to 63, as said below
- streamwise_positions: int32 [128], replicated, may hold values from 0 to 63, as said below
Outputs:
- advanced_composition: float32 [22, 128, 128, 512], P(None, 'gx', 'gy', 'sec')
- cond_means: float32 [22, 64, 64], P(None, 'gx')
Inputs may be any that keep to these rules, and one draw needn't show every extreme that they name: `mixture_classes`: bins of each plane cluster around a plane-dependent range. `streamwise_positions`: plane p has station ((p + h) // 2) mod 64 for one odd h between 1 and 7, so each station holds two axial planes.
All inputs are finite; a program needn't handle non-finite values.
Results may differ from a plain program's by a relative error of at most 0.0003.
Values sent between devices are 32-bit elements; how exact they have to be, the bound alone decides.
A program may use at most 64 MiB of HBM per device.

v0:
```python
import jax
import jax.numpy as jnp
from jax import lax
from jax.sharding import PartitionSpec as P

NB = 64


def extended(cells, sides, width):
    for axis, dim in sides:
        count = lax.axis_size(axis)
        ends = count - 1
        head = lax.slice_in_dim(cells, 0, width, axis=dim)
        tail = lax.slice_in_dim(cells, cells.shape[dim] - width, cells.shape[dim], axis=dim)
        cells = jnp.concatenate(
            [
                lax.ppermute(tail, axis, [(i, (i + 1) % count) for i in range(ends)]),
                cells,
                lax.ppermute(head, axis, [((i + 1) % count, i) for i in range(ends)]),
            ],
            axis=dim,
        )
    return cells


def neighbour(padded_composition, axis, start):
    index = [slice(None), slice(1, -1), slice(1, -1), slice(1, -1)]
    index[axis] = slice(start, start + padded_composition.shape[axis] - 2)
    return padded_composition[tuple(index)]


def kinetic_source_term(central_voxels, thermal_field, kinetics_jacobian):
    averaged_composition = jnp.einsum(
        "kj,jxyz->kxyz", kinetics_jacobian, central_voxels, precision=lax.Precision.HIGHEST
    )
    return 4.0 * jnp.exp(-2.0 / thermal_field) * averaged_composition


def on_device(
    composition_matrix,
    local_mixing_coefficient,
    thermal_field,
    component_mixing_weight,
    kinetics_jacobian,
    mixture_classes,
    streamwise_positions,
):
    collected_slabs = jnp.concatenate([composition_matrix, local_mixing_coefficient[None]], axis=0)
    padded_composition = extended(collected_slabs, (("sec", 3), ("gx", 1), ("gy", 2)), 1)
    reactive_yield_term = kinetic_source_term(composition_matrix, thermal_field, kinetics_jacobian)
    total = jnp.zeros_like(composition_matrix)
    for axis in (1, 2, 3):
        for start in (0, 2):
            other = neighbour(padded_composition, axis, start)
            total = total + 0.5 * (local_mixing_coefficient + other[-1]) * (
                other[:-1] - composition_matrix
            )
    advanced_composition = composition_matrix + 0.05 * (
        component_mixing_weight[:, None, None, None] * total + reactive_yield_term
    )
    planes = composition_matrix.shape[1]
    cells = composition_matrix.shape[2] * composition_matrix.shape[3]
    values = jnp.concatenate(
        [advanced_composition, jnp.ones_like(advanced_composition[:1])], axis=0
    )
    values = values.reshape(values.shape[0], planes, cells)
    levels = jnp.arange(NB, dtype=jnp.int32)
    onehot = (mixture_classes.reshape(planes, cells)[None] == levels[:, None, None]).astype(
        jnp.float32
    )
    partial_sums = jnp.einsum("kxc,bxc->kxb", values, onehot, precision=lax.Precision.HIGHEST)
    first_plane = lax.axis_index("gx") * planes
    own_stations = lax.dynamic_slice_in_dim(streamwise_positions, first_plane, planes)
    station_count = streamwise_positions.shape[0] // 2
    per_device = station_count // lax.axis_size("gx")
    owner = (own_stations[:, None] == jnp.arange(station_count, dtype=jnp.int32)[None]).astype(
        jnp.float32
    )
    tables = jnp.einsum("kxb,xs->ksb", partial_sums, owner, precision=lax.Precision.HIGHEST)
    whole = lax.psum(tables, ("sec", "gx", "gy"))
    totals = lax.dynamic_slice_in_dim(whole, lax.axis_index("gx") * per_device, per_device, 1)
    cond_means = totals[:-1] / jnp.maximum(totals[-1], 1.0)[None]
    return (advanced_composition, cond_means)


def solution(mesh):
    in_specs = (
        P(None, "gx", "gy", "sec"),
        P("gx", "gy", "sec"),
        P("gx", "gy", "sec"),
        P(),
        P(),
        P("gx", "gy", "sec"),
        P(),
    )
    out_specs = (P(None, "gx", "gy", "sec"), P(None, "gx", None))
    return jax.shard_map(
        on_device, mesh=mesh, in_specs=in_specs, out_specs=out_specs, check_vma=False
    )
```

profile of v0, /device:TPU:1, one launch (start us, length us, event | category | flops | bytes accessed | tf_op | source)
XLA Modules:
  0.0 367.0 jit_solution(12619638673433536906)
XLA Ops:
  7.2 2.4 fusion.13
  10.8 1.3 collective-permute-start.1
  13.2 5.7 %collective-permute-start = (f32[23,8,16,1]{0,2,3,1:T(8,128)S(1)}, f32[23,8,16,1]{0,2,3,1:T(8,128)S(1)}, u32[]{:S(2)}, u32[]{:S(2)}) collective-permute-start(f32[23,8,16,1]{0,2,3,1:T(8,128)S(1)} %copy.24), channel_id=1, source_target_pairs={{0,128},{128,256},{256,384},{1,129},{129,257},{257,385},{2,130},{1... | collective-permute-start | bytes 35336 | tf_op jit(solution)/shard_map/ppermute | solution.py:17
  18.9 1.5 copy.27
  20.5 2.4 copy.26
  22.9 2.3 pad_maximum_fusion.27
  25.2 5.5 %collective-permute-start.2 = (f32[23,1,16,130]{3,2,1,0:T(8,128)}, f32[23,1,16,130]{3,2,1,0:T(8,128)S(1)}, u32[]{:S(2)}, u32[]{:S(2)}) collective-permute-start(f32[23,1,16,130]{3,2,1,0:T(8,128)} %get-tuple-element.14), channel_id=1, source_target_pairs={{0,8},{8,16},{16,24},{24,32},{32,40},{40,48},{48,56},{56,64},{64,7... | collective-permute-start | bytes 574088 | tf_op jit(solution)/shard_map/ppermute | solution.py:17
  30.7 4.6 %collective-permute-start.3 = (f32[23,1,16,130]{3,2,1,0:T(8,128)}, f32[23,1,16,130]{3,2,1,0:T(8,128)}, u32[]{:S(2)}, u32[]{:S(2)}) collective-permute-start(f32[23,1,16,130]{3,2,1,0:T(8,128)} %get-tuple-element.15), channel_id=1, source_target_pairs={{8,0},{16,8},{24,16},{32,24},{40,32},{48,40},{56,48},{64,56},{72,6... | collective-permute-start | bytes 574088 | tf_op jit(solution)/shard_map/ppermute | solution.py:19
  35.5 2.0 copy.29
  38.2 2.0 copy.30
  40.2 1.7 pad_maximum_fusion.34
  42.0 2.3 pad_maximum_fusion.33
  44.3 1.3 collective-permute-start.4
  45.6 1.5 collective-permute-start.5
  47.9 2.8 collective-permute-done.4
  50.7 4.2 %collective-permute-done.5 = f32[23,10,1,130]{3,2,1,0:T(1,128)S(1)} collective-permute-done((f32[23,10,1,130]{3,2,1,0:T(1,128)S(1)}, f32[23,10,1,130]{3,2,1,0:T(1,128)S(1)}, u32[]{:S(2)}, u32[]{:S(2)}) %collective-permute-start.5) | collective-permute-done | bytes 119632 | tf_op jit(solution)/shard_map/ppermute | solution.py:19
  55.1 7.8 %fusion.17 = f32[22,8,16,128]{3,2,1,0:T(8,128)S(1)} fusion(f32[22,8,16,128]{3,2,1,0:T(8,128)S(1)} %copy-done.1, f32[23,8,16,1]{3,2,1,0:T(8,128)S(1)} %copy-done.2, f32[1,8,16,128]{3,2,1,0:T(8,128)S(1)} %bitcast.61, f32[23,10,1,130]{3,2,1,0:T(1,128)S(1)} %collective-permute-done.5, f32[23,1,16,130]{3,2,1,0:T(8,128)} %collective-permute-done.3, ...), kind=kLoop, calls=%fused_computation.21 | loop fusion | flops 12976128 | bytes 3922272 | tf_op jit(solution)/shard_map/add | solution.py:55
  62.9 4.3 %fusion.8 = f32[22,8,16,128]{3,0,2,1:T(8,128)S(1)} fusion(f32[23,8,16,1]{3,0,2,1:T(8,128)S(1)} %copy-done.4, f32[23,8,16,128]{3,0,2,1:T(8,128)S(1)} %copy-done.3, f32[22,8,16,128]{3,2,1,0:T(8,128)S(1)} %fusion.17, f32[22,8,16,128]{3,2,1,0:T(8,128)S(1)} %copy-done.1, f32[8,16,128]{2,1,0:T(8,128)S(1)} %exponential_multiply_fusion, ...), kind=kOutput, calls=%fused_computation.13 | convolution fusion | flops 98402304 | bytes 5977576 | tf_op jit(solution)/shard_map/kj,jxyz->kxyz/dot_general | solution.py:33
  68.7 2.6 reshape.20
  71.3 3.6 fusion.29
  74.9 1.5 convolution_bitcast_fusion
  76.4 1.4 copy.38
  77.8 280.2 %all-reduce.3.cloned.1.call-done = f32[23,64,64]{2,1,0:T(8,128)} async-done(((f32[23,64,64]{2,1,0:T(8,128)}), f32[23,64,64]{2,1,0:T(8,128)}) %all-reduce.3.cloned.1.call-update) | async-done | bytes 376848 | tf_op jit(solution)/shard_map/psum | solution.py:80
  358.7 1.5 dynamic-slice_divide_fusion
  (39 shorter events, 6.4 us)
Async XLA Ops:
  7.2 55.7 %copy-start = (f32[22,22]{1,0:T(8,128)S(1)}, f32[22,22]{1,0:T(8,128)}, u32[]{:S(2)}) copy-start(f32[22,22]{1,0:T(8,128)} %param.11) | copy-start | bytes 5812
  7.2 350.8 %all-reduce.3.cloned.1.call-start = ((), (), s32[]{:S(2)}) async-start(), calls=%async_computation | async-start | bytes 1507328 | tf_op jit(solution)/shard_map/psum | solution.py:80
  9.7 9.2 %copy-start.6 = (f32[8,16,128]{2,1,0:T(8,128)S(1)}, f32[8,16,128]{2,1,0:T(8,128)}, u32[]{:S(2)}) copy-start(f32[8,16,128]{2,1,0:T(8,128)} %param.9) | copy-start | bytes 196612
  10.8 8.1 %collective-permute-start.1 = (f32[23,8,16,1]{0,2,3,1:T(8,128)S(1)}, f32[23,8,16,1]{0,2,3,1:T(8,128)S(1)}, u32[]{:S(2)}, u32[]{:S(2)}) collective-permute-start(f32[23,8,16,1]{0,2,3,1:T(8,128)S(1)} %copy.25), channel_id=1, source_target_pairs={{128,0},{256,128},{384,256},{129,1},{257,129},{385,257},{130,2},{2... | collective-permute-start | bytes 35336 | tf_op jit(solution)/shard_map/ppermute | solution.py:19
  13.2 7.3 %collective-permute-start = (f32[23,8,16,1]{0,2,3,1:T(8,128)S(1)}, f32[23,8,16,1]{0,2,3,1:T(8,128)S(1)}, u32[]{:S(2)}, u32[]{:S(2)}) collective-permute-start(f32[23,8,16,1]{0,2,3,1:T(8,128)S(1)} %copy.24), channel_id=1, source_target_pairs={{0,128},{128,256},{256,384},{1,129},{129,257},{257,385},{2,130},{1... | collective-permute-start | bytes 35336 | tf_op jit(solution)/shard_map/ppermute | solution.py:17
  18.9 4.0 %copy-start.1 = (f32[22,8,16,128]{3,2,1,0:T(8,128)S(1)}, f32[22,8,16,128]{3,2,1,0:T(8,128)}, u32[]{:S(2)}) copy-start(f32[22,8,16,128]{3,2,1,0:T(8,128)} %param.7) | copy-start | bytes 4325380
  18.9 4.0 %copy-start.5 = (f32[8,16,128]{2,1,0:T(8,128)S(1)}, f32[8,16,128]{2,1,0:T(8,128)}, u32[]{:S(2)}) copy-start(f32[8,16,128]{2,1,0:T(8,128)} %param.8) | copy-start | bytes 196612
  25.2 16.8 %collective-permute-start.2 = (f32[23,1,16,130]{3,2,1,0:T(8,128)}, f32[23,1,16,130]{3,2,1,0:T(8,128)S(1)}, u32[]{:S(2)}, u32[]{:S(2)}) collective-permute-start(f32[23,1,16,130]{3,2,1,0:T(8,128)} %get-tuple-element.14), channel_id=1, source_target_pairs={{0,8},{8,16},{16,24},{24,32},{32,40},{40,48},{48,56},{56,64},{64,7... | collective-permute-start | bytes 574088 | tf_op jit(solution)/shard_map/ppermute | solution.py:17
  30.7 11.2 %collective-permute-start.3 = (f32[23,1,16,130]{3,2,1,0:T(8,128)}, f32[23,1,16,130]{3,2,1,0:T(8,128)}, u32[]{:S(2)}, u32[]{:S(2)}) collective-permute-start(f32[23,1,16,130]{3,2,1,0:T(8,128)} %get-tuple-element.15), channel_id=1, source_target_pairs={{8,0},{16,8},{24,16},{32,24},{40,32},{48,40},{56,48},{64,56},{72,6... | collective-permute-start | bytes 574088 | tf_op jit(solution)/shard_map/ppermute | solution.py:19
  35.4 2.1 copy-start.7
  35.4 2.7 copy-start.10
  40.2 1.7 copy-start.2
  44.3 6.4 %collective-permute-start.4 = (f32[23,10,1,130]{3,2,1,0:T(1,128)S(1)}, f32[23,10,1,130]{3,2,1,0:T(1,128)S(1)}, u32[]{:S(2)}, u32[]{:S(2)}) collective-permute-start(f32[23,10,1,130]{3,2,1,0:T(1,128)S(1)} %get-tuple-element.10), channel_id=1, source_target_pairs={{0,1},{1,2},{2,3},{3,4},{4,5},{5,6},{6,7},{8,9},{9,10},{10,11},{11... | collective-permute-start | bytes 358808 | tf_op jit(solution)/shard_map/ppermute | solution.py:17
  45.6 9.3 %collective-permute-start.5 = (f32[23,10,1,130]{3,2,1,0:T(1,128)S(1)}, f32[23,10,1,130]{3,2,1,0:T(1,128)S(1)}, u32[]{:S(2)}, u32[]{:S(2)}) collective-permute-start(f32[23,10,1,130]{3,2,1,0:T(1,128)S(1)} %get-tuple-element.11), channel_id=1, source_target_pairs={{1,0},{2,1},{3,2},{4,3},{5,4},{6,5},{7,6},{9,8},{10,9},{11,10},{12... | collective-permute-start | bytes 358808 | tf_op jit(solution)/shard_map/ppermute | solution.py:19
  55.0 7.8 %copy-start.3 = (f32[23,8,16,128]{3,0,2,1:T(8,128)S(1)}, f32[23,8,16,128]{3,0,2,1:T(8,128)}, u32[]{:S(2)}) copy-start(f32[23,8,16,128]{3,0,2,1:T(8,128)} %copy.29) | copy-start | bytes 4521988
  55.0 7.8 %copy-start.4 = (f32[23,8,16,1]{3,0,2,1:T(8,128)S(1)}, f32[23,8,16,1]{3,0,2,1:T(8,128)}, u32[]{:S(2)}) copy-start(f32[23,8,16,1]{3,0,2,1:T(8,128)} %copy.30) | copy-start | bytes 35332
  55.1 7.8 %copy-start.9 = (f32[22]{0:T(128)S(1)}, f32[22]{0:T(128)}, u32[]{:S(2)}) copy-start(f32[22]{0:T(128)} %param.10) | copy-start | bytes 268
  68.7 2.6 copy-start.8
Sparse Core Ops, SparseCore 0:
  76.5 281.4 all-reduce.2
where the time goes:
time: 368 us; the launch traced here: 367 us
  waiting for transfers between devices  287 us (78%)
  starting transfers between devices  19.9 us (5%)
  other arithmetic  19.8 us (5%)
  local copies, waits for them, and re-layouts  16.5 us (4%)
  between operations  14.3 us (4%)
  matrix products  9.33 us (3%)
    psum x1, waiting for transfers between devices, on_device(): whole = lax.psum(tables, ('sec', 'gx', 'gy'))  280 us
    ppermute x3, starting transfers between devices, extended(): lax.ppermute(tail, axis, [(i, (i + 1) % count) for i in range(ends)])  12.5 us
    add x1, other arithmetic, on_device(): total + 0.5 * (local_mixing_coefficient + other[-1]) * (other[:-1] - comp...  7.78 us
  transfers between devices with their start and end apart: 7, of which 3 were waited for; matrix products, arithmetic and copies ran while one was open for 3% of the time, Pallas kernels for 0%

commit v1 on v0

v1 whole, which is shorter than its diff:
```python
import functools

import jax
import jax.numpy as jnp
from jax import lax
from jax.experimental import pallas as pl
from jax.experimental.pallas import tpu as pltpu
from jax.sharding import PartitionSpec as P

NB = 64
YLO = 2
F32, BF16 = jnp.float32, jnp.bfloat16
MESH = pl.DeviceIdType.MESH
GROUPS = ((0,), (1, 2), (3, 4), (5, 6), (7,))


def kernel(
    species,
    comp_hbm,
    diff_hbm,
    temp_hbm,
    weight_hbm,
    jac_hbm,
    bins_hbm,
    pos_hbm,
    adv_hbm,
    cond_ref,
    u,
    adv,
    onehot,
    onehot_z,
    rate,
    temp,
    bins,
    jac,
    jac_pad,
    weight,
    pos,
    psum,
    zsend,
    zrecv,
    nxt,
    r1a,
    r1b,
    r2a,
    r2b,
    in_sem,
    out_sem,
    hs_sem,
    hr_sem,
    s1a,
    q1a,
    s1b,
    q1b,
    s2a,
    q2a,
    s2b,
    q2b,
):
    nsec, ngx, ngy = lax.axis_size("sec"), lax.axis_size("gx"), lax.axis_size("gy")
    nx, ny = ngy // YLO, nsec * YLO
    sec, gx, gy = lax.axis_index("sec"), lax.axis_index("gx"), lax.axis_index("gy")
    my_x, my_y = lax.rem(gy, nx), sec * YLO + gy // nx
    planes, rows = 8, 16
    dummy = species

    def device(s, i, g):
        return {"sec": s, "gx": i, "gy": g}

    def at_xy(i, x, y):
        return device(y // YLO, i, lax.rem(y, YLO) * nx + x)

    right, left = lax.rem(gx + 1, ngx), lax.rem(gx + ngx - 1, ngx)
    front, back = lax.rem(gy + 1, ngy), lax.rem(gy + ngy - 1, ngy)
    up, down = lax.rem(sec + 1, nsec), lax.rem(sec + nsec - 1, nsec)

    loads = [
        pltpu.make_async_copy(comp_hbm.at[s], u.at[1:9, 1:17, s, :], in_sem.at[s])
        for s in range(species)
    ]
    loads += [
        pltpu.make_async_copy(diff_hbm, u.at[1:9, 1:17, species + r, :], in_sem.at[species + r])
        for r in range(2)
    ]
    first = [
        pltpu.make_async_copy(bins_hbm, bins, in_sem.at[24]),
        pltpu.make_async_copy(temp_hbm, temp, in_sem.at[25]),
        pltpu.make_async_copy(jac_hbm, jac, in_sem.at[26]),
        pltpu.make_async_copy(weight_hbm, weight, in_sem.at[27]),
        pltpu.make_async_copy(pos_hbm, pos, in_sem.at[28]),
    ]
    for copy in first + loads:
        copy.start()

    barrier = pltpu.get_barrier_semaphore()
    peers = [device(sec, gx, front), device(sec, gx, back)]
    peers += [at_xy(gx, lax.rem(my_x + o, nx), my_y) for o in range(1, nx)]
    peers += [at_xy(gx, my_x, lax.rem(my_y + o, ny)) for o in range(1, ny)]
    for side in (right, left):
        peers += [at_xy(side, lax.rem(my_x + o, nx), my_y) for o in range(nx)]
        peers += [at_xy(side, my_x, lax.rem(my_y + o, ny)) for o in range(1, ny)]
    for peer in peers:
        pl.semaphore_signal(barrier, inc=1, device_id=peer, device_id_type=MESH)

    for copy in first:
        copy.wait()
    level = lax.broadcasted_iota(jnp.int32, (NB, 128), 0)

    def prepare(x, carry):
        for y in range(rows):
            row = bins[x, pl.ds(y, 1), :]
            onehot[x, :, y * 128 : (y + 1) * 128] = jnp.where(
                jnp.broadcast_to(row, (NB, 128)) == level, 1.0, 0.0
            ).astype(BF16)
        rate[x] = 0.2 * jnp.exp(-2.0 / temp[x])
        return carry

    lax.fori_loop(0, planes, prepare, 0)
    across = jnp.transpose(bins[...].reshape(planes * rows, 128).astype(F32))
    lane1 = lax.broadcasted_iota(jnp.int32, (1, 128), 1)
    group_of = (lane1 // rows + 1) // 2
    code_level = lax.broadcasted_iota(jnp.int32, (5 * NB, 128), 0)
    for side, lane in ((0, 0), (1, 127)):
        code = across[lane : lane + 1, :].astype(jnp.int32) + group_of * NB
        onehot_z[side] = jnp.where(
            jnp.broadcast_to(code, (5 * NB, 128)) == code_level, 1.0, 0.0
        ).astype(BF16)

    jac_pad[...] = jnp.zeros_like(jac_pad)
    jac_pad[0:species, 0:species] = jac[...]
    j_full = jac_pad[...]
    j_hi = j_full.astype(BF16)
    j_lo = (j_full - j_hi.astype(F32)).astype(BF16)
    row_id = lax.broadcasted_iota(jnp.int32, (24, 128), 0)
    lane_id = lax.broadcasted_iota(jnp.int32, (24, 128), 1)
    wk = jnp.zeros((24, 128), F32)
    for s in range(species):
        wk = jnp.where(row_id == s, 0.05 * weight[s], wk)

    for copy in loads:
        copy.wait()

    def pack(x, carry):
        low, high = carry
        for y in range(rows):
            j = x * rows + y
            turned = pltpu.roll(u[x + 1, y + 1], j, 1)
            low = jnp.where(lane_id == j, turned, low)
            high = jnp.where(lane_id == lax.rem(j + 127, 128), turned, high)
        return low, high

    blank = jnp.zeros((24, 128), F32)
    low, high = lax.fori_loop(0, planes, pack, (blank, blank))
    zsend[0] = low
    zsend[1] = pltpu.roll(high, 1, 1)

    pl.semaphore_wait(barrier, len(peers))

    def remote(src, dst, send, recv, peer):
        return pltpu.make_async_remote_copy(
            src_ref=src, dst_ref=dst, send_sem=send, recv_sem=recv, device_id=peer,
            device_id_type=MESH,
        )

    halo = [
        remote(u.at[8, 1:17], u.at[0, 1:17], hs_sem.at[0], hr_sem.at[0], device(sec, right, gy)),
        remote(u.at[1, 1:17], u.at[9, 1:17], hs_sem.at[1], hr_sem.at[1], device(sec, left, gy)),
        remote(u.at[1:9, 16], u.at[1:9, 0], hs_sem.at[2], hr_sem.at[2], device(sec, gx, front)),
        remote(u.at[1:9, 1], u.at[1:9, 17], hs_sem.at[3], hr_sem.at[3], device(sec, gx, back)),
        remote(zsend.at[1], zrecv.at[0], hs_sem.at[4], hr_sem.at[4], device(up, gx, gy)),
        remote(zsend.at[0], zrecv.at[1], hs_sem.at[5], hr_sem.at[5], device(down, gx, gy)),
    ]
    for copy in halo:
        copy.start()

    def dot(a, b):
        return lax.dot_general(a, b, (((1,), (0,)), ((), ())), preferred_element_type=F32)

    def dot_t(a, b):
        return lax.dot_general(a, b, (((1,), (1,)), ((), ())), preferred_element_type=F32)

    def binned(values, hot):
        hi = values.astype(BF16)
        lo = (values - hi.astype(F32)).astype(BF16)
        return dot_t(hi, hot) + dot_t(lo, hot)

    not_last, not_first = lane1 < 127, lane1 > 0

    def inner(x, carry):
        whole = jnp.concatenate([u[x + 1, y + 1] for y in range(rows)], axis=1)
        hi = whole.astype(BF16)
        lo = (whole - hi.astype(F32)).astype(BF16)
        source = dot(j_hi, hi) + dot(j_hi, lo) + dot(j_lo, hi)
        done = []
        xm, xp = jnp.maximum(x, 1), jnp.minimum(x + 2, 8)
        for y in range(rows):
            c = u[x + 1, y + 1]
            d = c[dummy : dummy + 1]
            flux = None
            for other in (
                u[xm, y + 1],
                u[xp, y + 1],
                u[x + 1, max(y, 1)],
                u[x + 1, min(y + 2, 16)],
            ):
                term = (0.5 * (d + other[dummy : dummy + 1])) * (other - c)
                flux = term if flux is None else flux + term
            for turn, keep in ((127, not_last), (1, not_first)):
                other = pltpu.roll(c, turn, 1)
                half = jnp.where(keep, 0.5 * (d + other[dummy : dummy + 1]), 0.0)
                flux = flux + half * (other - c)
            part = source[:, y * 128 : (y + 1) * 128]
            value = c + wk * flux + rate[x, pl.ds(y, 1), :] * part
            adv[x, y] = value
            done.append(jnp.where(row_id == dummy, 1.0, value))
        psum[x] = binned(jnp.concatenate(done, axis=1), onehot[x])
        return carry

    lax.fori_loop(0, planes, inner, 0)

    for copy in halo:
        copy.wait()

    def face(c, other, inside):
        gate = jnp.where(inside, 1.0, 0.0)
        other = other * gate
        return wk * (0.5 * (c[dummy : dummy + 1] + other[dummy : dummy + 1]) * (other - c))

    for x, ghost, inside in ((0, 0, gx > 0), (7, 9, gx < ngx - 1)):
        terms = []
        for y in range(rows):
            term = face(u[x + 1, y + 1], u[ghost, y + 1], inside)
            adv[x, y] = adv[x, y] + term
            terms.append(term)
        psum[x] = psum[x] + binned(jnp.concatenate(terms, axis=1), onehot[x])

    def faces_y(x, carry):
        total = psum[x]
        for y, ghost, inside in ((0, 0, gy > 0), (15, 17, gy < ngy - 1)):
            term = face(u[x + 1, y + 1], u[x + 1, ghost], inside)
            adv[x, y] = adv[x, y] + term
            total = total + binned(term, onehot[x, :, y * 128 : (y + 1) * 128])
        psum[x] = total
        return carry

    lax.fori_loop(0, planes, faces_y, 0)
    ends = [
        face(zsend[0], zrecv[0], sec > 0),
        face(zsend[1], zrecv[1], sec < nsec - 1),
    ]
    by_group = binned(ends[0], onehot_z[0]) + binned(ends[1], onehot_z[1])

    count = pos.shape[0] // 2
    per = count // ngx
    sums = []
    for g, members in enumerate(GROUPS):
        total = by_group[:, g * NB : (g + 1) * NB]
        for x in members:
            total = total + psum[x]
        sums.append((pos[gx * planes + members[0]], total))

    def table(slot):
        target = lax.rem(gx * per + slot, count)
        out = jnp.zeros((24, NB), F32)
        for station, total in sums:
            out = out + jnp.where(station == target, 1.0, 0.0) * total
        return out

    slots = [table(s) for s in range(2 * per)]
    r1a[0, my_x] = jnp.concatenate(slots[0:2], axis=1)
    r1b[0, my_y] = jnp.concatenate(slots[2:4], axis=1)
    nxt[0] = jnp.concatenate(slots[4:6], axis=1)
    nxt[1] = jnp.concatenate(slots[6:8], axis=1)

    waits = []
    for o in range(ny):
        y = lax.rem(my_y + o, ny)
        if o:
            c = remote(r1b.at[0, my_y], r1b.at[0, my_y], s1b.at[0, o], q1b.at[0, my_y], at_xy(gx, my_x, y))
            c.start()
            waits.append(c)
        c = remote(nxt.at[1], r1b.at[1, my_y], s1b.at[1, o], q1b.at[1, my_y], at_xy(right, my_x, y))
        c.start()
        waits.append(c)
    for o in range(nx):
        x = lax.rem(my_x + o, nx)
        if o:
            c = remote(r1a.at[0, my_x], r1a.at[0, my_x], s1a.at[0, o], q1a.at[0, my_x], at_xy(gx, x, my_y))
            c.start()
            waits.append(c)
        c = remote(nxt.at[0], r1a.at[1, my_x], s1a.at[1, o], q1a.at[1, my_x], at_xy(right, x, my_y))
        c.start()
        waits.append(c)

    def ends_in(x, carry):
        a, b = carry
        for y in range(rows):
            j = x * rows + y
            head = pltpu.roll(a, lax.rem(128 - j, 128), 1)
            tail = pltpu.roll(b, lax.rem(255 - j, 128), 1)
            adv[x, y] = adv[x, y] + jnp.where(
                lane_id == 0, head, jnp.where(lane_id == 127, tail, 0.0)
            )
        return carry

    lax.fori_loop(0, planes, ends_in, (ends[0], ends[1]))
    outs = [
        pltpu.make_async_copy(adv.at[:, :, s, :], adv_hbm.at[s], out_sem.at[s])
        for s in range(species)
    ]
    for copy in outs:
        copy.start()

    def arrived(buffer, sem):
        pltpu.make_async_copy(buffer, buffer, sem).wait()

    def gather(buffer, sems, mine, size, layers):
        for o in range(size):
            slot = lax.rem(mine + o, size)
            for layer in range(layers):
                if layer or o:
                    arrived(buffer.at[layer, slot], sems.at[layer, slot])
        total = buffer[0, 0]
        for layer in range(layers):
            for slot in range(size):
                if layer or slot:
                    total = total + buffer[layer, slot]
        return total

    r2a[0, my_y] = gather(r1a, q1a, my_x, nx, 2)
    for o in range(1, ny):
        y = lax.rem(my_y + o, ny)
        c = remote(r2a.at[0, my_y], r2a.at[0, my_y], s2a.at[0, o], q2a.at[0, my_y], at_xy(gx, my_x, y))
        c.start()
        waits.append(c)
    r2b[0, my_x] = gather(r1b, q1b, my_y, ny, 2)
    for o in range(1, nx):
        x = lax.rem(my_x + o, nx)
        c = remote(r2b.at[0, my_x], r2b.at[0, my_x], s2b.at[0, o], q2b.at[0, my_x], at_xy(gx, x, my_y))
        c.start()
        waits.append(c)
    halves = [gather(r2a, q2a, my_y, ny, 1), gather(r2b, q2b, my_x, nx, 1)]
    for half in range(2):
        whole = halves[half]
        means = whole / jnp.maximum(whole[dummy : dummy + 1], 1.0)
        for part in range(2):
            cond_ref[:, 2 * half + part, :] = means[0:species, part * NB : (part + 1) * NB]
    for copy in waits:
        copy.wait_send()
    for copy in outs:
        copy.wait()


def on_device(comp, diff, temp, weight, jac, bins, pos):
    species, planes, rows, cells = comp.shape
    nx = lax.axis_size("gy") // YLO
    ny = lax.axis_size("sec") * YLO
    per = pos.shape[0] // 2 // lax.axis_size("gx")
    dma = pltpu.SemaphoreType.DMA
    anywhere = pl.BlockSpec(memory_space=pl.ANY)
    return pl.pallas_call(
        functools.partial(kernel, species),
        out_shape=(
            jax.ShapeDtypeStruct(comp.shape, F32),
            jax.ShapeDtypeStruct((species, per, NB), F32),
        ),
        in_specs=[anywhere] * 7,
        out_specs=(anywhere, pl.BlockSpec(memory_space=pltpu.VMEM)),
        scratch_shapes=[
            pltpu.VMEM((planes + 2, rows + 2, 24, cells), F32),
            pltpu.VMEM((planes, rows, 24, cells), F32),
            pltpu.VMEM((planes, NB, rows * cells), BF16),
            pltpu.VMEM((2, 5 * NB, cells), BF16),
            pltpu.VMEM((planes, rows, cells), F32),
            pltpu.VMEM((planes, rows, cells), F32),
            pltpu.VMEM((planes, rows, cells), jnp.int32),
            pltpu.VMEM(jac.shape, F32),
            pltpu.VMEM((24, 24), F32),
            pltpu.SMEM(weight.shape, F32),
            pltpu.SMEM(pos.shape, jnp.int32),
            pltpu.VMEM((planes, 24, NB), F32),
            pltpu.VMEM((2, 24, cells), F32),
            pltpu.VMEM((2, 24, cells), F32),
            pltpu.VMEM((2, 24, 2 * NB), F32),
            pltpu.VMEM((2, nx, 24, 2 * NB), F32),
            pltpu.VMEM((2, ny, 24, 2 * NB), F32),
            pltpu.VMEM((1, ny, 24, 2 * NB), F32),
            pltpu.VMEM((1, nx, 24, 2 * NB), F32),
            dma((29,)),
            dma((species,)),
            dma((6,)),
            dma((6,)),
            dma((2, nx)),
            dma((2, nx)),
            dma((2, ny)),
            dma((2, ny)),
            dma((1, ny)),
            dma((1, ny)),
            dma((1, nx)),
            dma((1, nx)),
        ],
        compiler_params=pltpu.CompilerParams(collective_id=0, has_side_effects=True),
        name="section",
    )(comp, diff, temp, weight, jac, bins, pos)


def solution(mesh):
    in_specs = (
        P(None, "gx", "gy", "sec"),
        P("gx", "gy", "sec"),
        P("gx", "gy", "sec"),
        P(),
        P(),
        P("gx", "gy", "sec"),
        P(),
    )
    out_specs = (P(None, "gx", "gy", "sec"), P(None, "gx", None))
    return jax.shard_map(
        on_device, mesh=mesh, in_specs=in_specs, out_specs=out_specs, check_vma=False
    )
```

time: 368 us -> 39 us (0.11)
  the two profiles are of different devices: /device:TPU:1 before, /device:TPU:16 now
where the time goes in v1:
time: 39 us; the launch traced here: 38.8 us
  Pallas kernels  34.9 us (89%)
  local copies, waits for them, and re-layouts  3.24 us (8%)
  between operations  0.65 us (2%)
    pallas_call x1, Pallas kernels, on_device(): pl.pallas_call(functools.partial(kernel, species), out_shape=(jax.ShapeDt...  34.9 us
    unnamed x4, local copies, waits for them, and re-layouts  3.24 us

profile of v1, /device:TPU:16, one launch (start us, length us, event | category | flops | bytes accessed | tf_op | source)
XLA Modules:
  0.0 38.8 jit_solution(5504653005846631735)
XLA Ops:
  0.6 34.9 %section.1 = (f32[22,8,16,128]{3,2,1,0:T(8,128)}, f32[22,4,64]{2,1,0:T(4,128)}) custom-call(f32[22,8,16,128]{3,2,1,0:T(8,128)} %comp_hbm.1, f32[8,16,128]{2,1,0:T(8,128)} %diff_hbm.1, f32[8,16,128]{2,1,0:T(8,128)} %temp_hbm.1, f32[22]{0:T(128)} %weight_hbm.1, f32[22,22]{1,0:T(8,128)} %jac_hbm.1, s32[8,16,128]{2,1,0:T(8,128)} %bins_hbm.1, s32[128]{0:T(128)} %pos_hbm.1), custom_call_target="tpu_custom_call" | custom-call | tf_op jit(solution)/shard_map/section/pallas_call | solution.py:361
  35.5 0.0 copy-start
  35.5 2.6 %copy.11 = f32[22,8,16,128]{3,2,1,0:T(8,128)} copy(f32[22,8,16,128]{3,2,1,0:T(8,128)} %get-tuple-element.4) | data formatting | bytes 2883584
  38.1 0.0 copy-done
  38.1 0.6 %copy.12 = f32[22,4,64]{2,1,0:T(4,128)} copy(f32[22,4,64]{2,1,0:T(4,128)S(1)} %copy-done) | data formatting | bytes 45056
Async XLA Ops:
  35.5 2.6 %copy-start = (f32[22,4,64]{2,1,0:T(4,128)S(1)}, f32[22,4,64]{2,1,0:T(4,128)}, u32[]{:S(2)}) copy-start(f32[22,4,64]{2,1,0:T(4,128)} %get-tuple-element.5) | copy-start | bytes 67588

commit v2 on v1

v2 whole, which is shorter than its diff:
```python
import functools

import jax
import jax.numpy as jnp
from jax import lax
from jax.experimental import pallas as pl
from jax.experimental.pallas import tpu as pltpu
from jax.sharding import PartitionSpec as P

NB = 64
YLO = 2
ROWS = 24
F32, BF16 = jnp.float32, jnp.bfloat16
MESH = pl.DeviceIdType.MESH
GROUPS = ((0,), (1, 2), (3, 4), (5, 6), (7,))


def remote(src, dst, send, recv, peer):
    return pltpu.make_async_remote_copy(
        src_ref=src, dst_ref=dst, send_sem=send, recv_sem=recv, device_id=peer, device_id_type=MESH
    )


def split(values):
    hi = values.astype(BF16).astype(F32)
    return jnp.concatenate([hi, values - hi], axis=0).astype(BF16)


def binned(values, hot):
    both = lax.dot_general(
        split(values), hot, (((1,), (1,)), ((), ())), preferred_element_type=F32
    )
    return both[0:ROWS] + both[ROWS : 2 * ROWS]


def kernel(
    species,
    comp_hbm,
    diff_hbm,
    temp_hbm,
    weight_hbm,
    jac_hbm,
    bins_hbm,
    pos_hbm,
    adv,
    sums,
    u,
    onehot,
    onehot_z,
    rate,
    flux_x,
    temp,
    bins,
    jac,
    jac_pad,
    weight,
    pos,
    psum,
    zsend,
    zrecv,
    r1a,
    r1b,
    next_a,
    next_b,
    r2a,
    r2b,
    in_sem,
    hs_sem,
    hr_sem,
    s1a,
    q1a,
    s1b,
    q1b,
    s2a,
    q2a,
    s2b,
    q2b,
    ready,
):
    nsec, ngx, ngy = lax.axis_size("sec"), lax.axis_size("gx"), lax.axis_size("gy")
    nx, ny = ngy // YLO, nsec * YLO
    sec, gx, gy = lax.axis_index("sec"), lax.axis_index("gx"), lax.axis_index("gy")
    my_x, my_y = lax.rem(gy, nx), sec * YLO + gy // nx
    planes, rows = 8, 16
    dif = species

    def device(s, i, g):
        return {"sec": s, "gx": i, "gy": g}

    def at_xy(i, x, y):
        return device(y // YLO, i, lax.rem(y, YLO) * nx + x)

    right, left = lax.rem(gx + 1, ngx), lax.rem(gx + ngx - 1, ngx)
    front, back = lax.rem(gy + 1, ngy), lax.rem(gy + ngy - 1, ngy)
    up, down = lax.rem(sec + 1, nsec), lax.rem(sec + nsec - 1, nsec)

    loads = [
        pltpu.make_async_copy(comp_hbm.at[s], u.at[1:9, 1:17, s, :], in_sem.at[s])
        for s in range(species)
    ]
    loads.append(pltpu.make_async_copy(diff_hbm, u.at[1:9, 1:17, dif, :], in_sem.at[species]))
    first = [
        pltpu.make_async_copy(bins_hbm, bins, in_sem.at[24]),
        pltpu.make_async_copy(temp_hbm, temp, in_sem.at[25]),
        pltpu.make_async_copy(jac_hbm, jac, in_sem.at[26]),
        pltpu.make_async_copy(weight_hbm, weight, in_sem.at[27]),
        pltpu.make_async_copy(pos_hbm, pos, in_sem.at[28]),
    ]
    for copy in loads:
        copy.start()

    barrier = pltpu.get_barrier_semaphore()
    peers = [
        device(sec, right, gy),
        device(sec, left, gy),
        device(sec, gx, front),
        device(sec, gx, back),
        device(up, gx, gy),
        device(down, gx, gy),
        at_xy(gx, lax.rem(my_x + 1, nx), my_y),
        at_xy(gx, lax.rem(my_x + nx - 1, nx), my_y),
        at_xy(gx, my_x, lax.rem(my_y + 1, ny)),
        at_xy(gx, my_x, lax.rem(my_y + ny - 1, ny)),
    ]
    for peer in peers:
        pl.semaphore_signal(barrier, inc=1, device_id=peer, device_id_type=MESH)
    for copy in first:
        copy.start()

    ones = jnp.ones((1, 128), F32)
    level = lax.broadcasted_iota(jnp.int32, (NB, 128), 0)
    for copy in first:
        copy.wait()

    def prepare(x, carry):
        for y in range(rows):
            row = bins[x, pl.ds(y, 1), :]
            onehot[x, :, y * 128 : (y + 1) * 128] = jnp.where(
                jnp.broadcast_to(row, (NB, 128)) == level, 1.0, 0.0
            ).astype(BF16)
            u[x + 1, y + 1, dif + 1 : dif + 2, :] = ones
        rate[x] = 0.2 * jnp.exp(-2.0 / temp[x])
        return carry

    lax.fori_loop(0, planes, prepare, 0)
    flux_x[...] = jnp.zeros_like(flux_x)
    jac_pad[...] = jnp.zeros_like(jac_pad)
    jac_pad[0:species, 0:species] = jac[...]
    j_full = jac_pad[...]
    j_hi = j_full.astype(BF16).astype(F32)
    j_lo = j_full - j_hi
    j_all = jnp.concatenate([j_hi, j_hi, j_lo, j_lo], axis=1).astype(BF16)
    row_id = lax.broadcasted_iota(jnp.int32, (ROWS, 128), 0)
    lane_id = lax.broadcasted_iota(jnp.int32, (ROWS, 128), 1)
    wk = jnp.zeros((ROWS, 128), F32)
    for s in range(species):
        wk = jnp.where(row_id == s, 0.025 * weight[s], wk)

    for copy in loads:
        copy.wait()
    pl.semaphore_wait(barrier, len(peers))
    halo = [
        remote(u.at[8, 1:17], u.at[0, 1:17], hs_sem.at[0], hr_sem.at[0], device(sec, right, gy)),
        remote(u.at[1, 1:17], u.at[9, 1:17], hs_sem.at[1], hr_sem.at[1], device(sec, left, gy)),
        remote(u.at[1:9, 16], u.at[1:9, 0], hs_sem.at[2], hr_sem.at[2], device(sec, gx, front)),
        remote(u.at[1:9, 1], u.at[1:9, 17], hs_sem.at[3], hr_sem.at[3], device(sec, gx, back)),
        remote(zsend.at[1], zrecv.at[0], hs_sem.at[4], hr_sem.at[4], device(up, gx, gy)),
        remote(zsend.at[0], zrecv.at[1], hs_sem.at[5], hr_sem.at[5], device(down, gx, gy)),
    ]
    for copy in halo[0:4]:
        copy.start()

    def pack(x, carry):
        low, high = carry
        heads = tails = None
        for y in range(rows):
            c = u[x + 1, y + 1]
            turned = pltpu.roll(c, y, 1) if y else c
            heads = turned if y == 0 else jnp.where(lane_id == y, turned, heads)
            tails = turned if y == 0 else jnp.where(lane_id == y - 1, turned, tails)
        here = lane_id // rows == x
        low = jnp.where(here, pltpu.roll(heads, x * rows, 1), low)
        high = jnp.where(here, pltpu.roll(tails, x * rows + 1, 1), high)
        return low, high

    blank = jnp.zeros((ROWS, 128), F32)
    low, high = lax.fori_loop(0, planes, pack, (blank, blank))
    zsend[0] = low
    zsend[1] = high
    for copy in halo[4:6]:
        copy.start()

    across = jnp.transpose(bins[...].reshape(planes * rows, 128).astype(F32))
    lane1 = lax.broadcasted_iota(jnp.int32, (1, 128), 1)
    group_of = (lane1 // rows + 1) // 2
    code_level = lax.broadcasted_iota(jnp.int32, (5 * NB, 128), 0)
    for side, lane in ((0, 0), (1, 127)):
        code = across[lane : lane + 1, :].astype(jnp.int32) + group_of * NB
        onehot_z[side] = jnp.where(
            jnp.broadcast_to(code, (5 * NB, 128)) == code_level, 1.0, 0.0
        ).astype(BF16)

    inside = lax.broadcasted_iota(jnp.int32, (1, 128), 1) < 127

    def inner(x, carry):
        parts = split(jnp.concatenate([u[x + 1, y + 1] for y in range(rows)], axis=1))
        source = jnp.dot(
            j_all, jnp.concatenate([parts, parts], axis=0), preferred_element_type=F32
        )
        done = []
        xp = jnp.minimum(x + 2, 8)
        flux_y = None
        for y in range(rows):
            c = u[x + 1, y + 1]
            d = u[x + 1, y + 1, dif : dif + 1, :]
            after = (d + u[xp, y + 1, dif : dif + 1, :]) * (u[xp, y + 1] - c)
            flux = after - flux_x[y]
            flux_x[y] = after
            if y < rows - 1:
                later = (d + u[x + 1, y + 2, dif : dif + 1, :]) * (u[x + 1, y + 2] - c)
                flux = flux + (later if flux_y is None else later - flux_y)
                flux_y = later
            else:
                flux = flux - flux_y
            turned = pltpu.roll(c, 127, 1)
            gain = jnp.where(inside, d + pltpu.roll(d, 127, 1), 0.0)
            out = gain * (turned - c)
            flux = flux + (out - pltpu.roll(out, 1, 1))
            part = source[:, y * 128 : (y + 1) * 128]
            value = (c + rate[x, pl.ds(y, 1), :] * part) + wk * flux
            adv[x, y] = value
            done.append(value)
        psum[x] = binned(jnp.concatenate(done, axis=1), onehot[x])
        return carry

    lax.fori_loop(0, planes, inner, 0)

    for copy in halo:
        copy.wait_recv()
    near = [at_xy(gx, lax.rem(my_x + o, nx), my_y) for o in range(1, nx)]
    near += [at_xy(gx, my_x, lax.rem(my_y + o, ny)) for o in range(1, ny)]
    for peer in near:
        pl.semaphore_signal(ready, inc=1, device_id=peer, device_id_type=MESH)

    def face(c, d, other, d_other, gate):
        return wk * ((d + d_other * gate) * (other * gate - c))

    def gate_of(there):
        return jnp.where(there, 1.0, 0.0)

    faces_x = []
    for x, ghost, gate in ((0, 0, gate_of(gx > 0)), (7, 9, gate_of(gx < ngx - 1))):
        terms = []
        for y in range(rows):
            term = face(
                u[x + 1, y + 1],
                u[x + 1, y + 1, dif : dif + 1, :],
                u[ghost, y + 1],
                u[ghost, y + 1, dif : dif + 1, :],
                gate,
            )
            adv[x, y] = adv[x, y] + term
            terms.append(term)
        faces_x.append(binned(jnp.concatenate(terms, axis=1), onehot[x]))

    gate_back, gate_front = gate_of(gy > 0), gate_of(gy < ngy - 1)
    plane_sums = []
    for x in range(planes):
        terms = []
        for y, ghost, gate in ((0, 0, gate_back), (15, 17, gate_front)):
            term = face(
                u[x + 1, y + 1],
                u[x + 1, y + 1, dif : dif + 1, :],
                u[x + 1, ghost],
                u[x + 1, ghost, dif : dif + 1, :],
                gate,
            )
            adv[x, y] = adv[x, y] + term
            terms.append(term)
        hot = jnp.concatenate([onehot[x, :, 0:128], onehot[x, :, 15 * 128 : 16 * 128]], axis=1)
        total = psum[x] + binned(jnp.concatenate(terms, axis=1), hot)
        if x in (0, 7):
            total = total + faces_x[x // 7]
        plane_sums.append(total)
    ends = []
    for side, gate in ((0, gate_of(sec > 0)), (1, gate_of(sec < nsec - 1))):
        c, other = zsend[side], zrecv[side]
        ends.append(face(c, c[dif : dif + 1], other, other[dif : dif + 1], gate))
    by_group = binned(ends[0], onehot_z[0]) + binned(ends[1], onehot_z[1])

    totals = []
    for g, members in enumerate(GROUPS):
        total = by_group[:, g * NB : (g + 1) * NB]
        for x in members:
            total = total + plane_sums[x]
        totals.append(total)
    totals.append(jnp.zeros_like(totals[0]))
    for k in range(3):
        pair = jnp.concatenate(totals[2 * k : 2 * k + 2], axis=1)
        r1b[0, my_y, :, k * 128 : (k + 1) * 128] = pair[8:24]
        r1a[0, my_x, :, k * 128 : (k + 1) * 128] = pair[0:8]

    waits = []

    def send(src, dst, sem, recv, peer):
        copy = remote(src, dst, sem, recv, peer)
        copy.start()
        waits.append(copy)

    far_y = sorted(range(1, ny), key=lambda o: -min(o, ny - o))
    far_x = sorted(range(1, nx), key=lambda o: -min(o, nx - o))
    for o in far_y:
        block = r1b.at[0, my_y]
        send(block, block, s1b.at[0, o], q1b.at[0, my_y], at_xy(gx, my_x, lax.rem(my_y + o, ny)))
    for o in far_x:
        block = r1a.at[0, my_x]
        send(block, block, s1a.at[0, o], q1a.at[0, my_x], at_xy(gx, lax.rem(my_x + o, nx), my_y))

    def ends_in(x, carry):
        a, b = carry
        a = pltpu.roll(a, lax.rem(128 - x * rows, 128), 1)
        b = pltpu.roll(b, 127 - x * rows, 1)
        for y in range(rows):
            head = pltpu.roll(a, 128 - y, 1) if y else a
            tail = pltpu.roll(b, 128 - y, 1) if y else b
            adv[x, y] = adv[x, y] + jnp.where(
                lane_id == 0, head, jnp.where(lane_id == 127, tail, 0.0)
            )
        return carry

    lax.fori_loop(0, planes, ends_in, (ends[0], ends[1]))

    def arrived(buffer, sem):
        pltpu.make_async_copy(buffer, buffer, sem).wait()

    def gather(buffer, sems, mine, size, layers):
        for o in range(size):
            slot = lax.rem(mine + o, size)
            for layer in range(layers):
                if layer or o:
                    arrived(buffer.at[layer, slot], sems.at[layer, slot])
        total = buffer[0, 0]
        for layer in range(layers):
            for slot in range(size):
                if layer or slot:
                    total = total + buffer[layer, slot]
        return total

    count = pos.shape[0] // 2
    per = count // ngx
    m = lax.rem(pos[gx * planes] - gx * per + count, count)

    def stations(total):
        p = [total[:, k * 128 : (k + 1) * 128] for k in range(3)]
        turned = [pltpu.roll(v, NB, 1) for v in p]
        high = lax.broadcasted_iota(jnp.int32, p[0].shape, 1) >= NB
        q = [jnp.where(high, turned[k], turned[k - 1] if k else 0.0) for k in range(3)]
        flag = [jnp.where(m == k, 1.0, 0.0) for k in range(4)]
        zero = jnp.zeros_like(p[0])
        shifted = (p + [zero], q + [zero], [zero] + p, [zero] + q)
        out = []
        for k in range(4):
            out.append(sum(flag[i] * shifted[i][k] for i in range(4)))
        return jnp.concatenate(out[0:2], axis=1), jnp.concatenate(out[2:4], axis=1)

    own, following = stations(gather(r1a, q1a, my_x, nx, 1))
    r2a[0, my_y] = own
    next_a[...] = following
    pl.semaphore_wait(ready, len(near))
    for o in far_y + [0]:
        peer = lax.rem(my_y + o, ny)
        send(next_a, r2a.at[1, my_y], s2a.at[1, o], q2a.at[1, my_y], at_xy(right, my_x, peer))
        if o:
            block = r2a.at[0, my_y]
            send(block, block, s2a.at[0, o], q2a.at[0, my_y], at_xy(gx, my_x, peer))
    own, following = stations(gather(r1b, q1b, my_y, ny, 1))
    r2b[0, my_x] = own
    next_b[...] = following
    for o in far_x + [0]:
        peer = lax.rem(my_x + o, nx)
        send(next_b, r2b.at[1, my_x], s2b.at[1, o], q2b.at[1, my_x], at_xy(right, peer, my_y))
        if o:
            block = r2b.at[0, my_x]
            send(block, block, s2b.at[0, o], q2b.at[0, my_x], at_xy(gx, peer, my_y))
    for copy in halo + waits:
        copy.wait_send()
    sums[8:24] = gather(r2b, q2b, my_x, nx, 2)
    sums[0:8] = gather(r2a, q2a, my_y, ny, 2)


def finish(adv, sums, adv_hbm, cond_ref, out_sem):
    species = adv_hbm.shape[0]
    outs = [
        pltpu.make_async_copy(adv.at[:, :, s, :], adv_hbm.at[s], out_sem.at[s])
        for s in range(species)
    ]
    for copy in outs:
        copy.start()
    whole = sums[...]
    means = whole / jnp.maximum(whole[ROWS - 1 : ROWS], 1.0)
    for part in range(4):
        cond_ref[:, part, :] = means[0:species, part * NB : (part + 1) * NB]
    for copy in outs:
        copy.wait()


def on_device(comp, diff, temp, weight, jac, bins, pos):
    species, planes, rows, cells = comp.shape
    nx = lax.axis_size("gy") // YLO
    ny = lax.axis_size("sec") * YLO
    per = pos.shape[0] // 2 // lax.axis_size("gx")
    dma = pltpu.SemaphoreType.DMA
    anywhere = pl.BlockSpec(memory_space=pltpu.HBM)
    vmem = pl.BlockSpec(memory_space=pltpu.VMEM)
    adv, sums = pl.pallas_call(
        functools.partial(kernel, species),
        out_shape=(
            pltpu.VMEM((planes, rows, ROWS, cells), F32),
            pltpu.VMEM((ROWS, 4 * NB), F32),
        ),
        in_specs=[anywhere] * 7,
        out_specs=(vmem, vmem),
        scratch_shapes=[
            pltpu.VMEM((planes + 2, rows + 2, ROWS, cells), F32),
            pltpu.VMEM((planes, NB, rows * cells), BF16),
            pltpu.VMEM((2, 5 * NB, cells), BF16),
            pltpu.VMEM((planes, rows, cells), F32),
            pltpu.VMEM((rows, ROWS, cells), F32),
            pltpu.VMEM((planes, rows, cells), F32),
            pltpu.VMEM((planes, rows, cells), jnp.int32),
            pltpu.VMEM(jac.shape, F32),
            pltpu.VMEM((ROWS, ROWS), F32),
            pltpu.SMEM(weight.shape, F32),
            pltpu.SMEM(pos.shape, jnp.int32),
            pltpu.VMEM((planes, ROWS, NB), F32),
            pltpu.VMEM((2, ROWS, cells), F32),
            pltpu.VMEM((2, ROWS, cells), F32),
            pltpu.VMEM((1, nx, 8, 6 * NB), F32),
            pltpu.VMEM((1, ny, 16, 6 * NB), F32),
            pltpu.VMEM((8, 4 * NB), F32),
            pltpu.VMEM((16, 4 * NB), F32),
            pltpu.VMEM((2, ny, 8, 4 * NB), F32),
            pltpu.VMEM((2, nx, 16, 4 * NB), F32),
            dma((29,)),
            dma((6,)),
            dma((6,)),
            dma((1, nx)),
            dma((1, nx)),
            dma((1, ny)),
            dma((1, ny)),
            dma((2, ny)),
            dma((2, ny)),
            dma((2, nx)),
            dma((2, nx)),
            pltpu.SemaphoreType.REGULAR,
        ],
        compiler_params=pltpu.CompilerParams(
            collective_id=0, has_side_effects=True, vmem_limit_bytes=65420000
        ),
        name="section",
    )(comp, diff, temp, weight, jac, bins, pos)
    return pl.pallas_call(
        finish,
        out_shape=(
            jax.ShapeDtypeStruct(comp.shape, F32),
            jax.ShapeDtypeStruct((species, per, NB), F32),
        ),
        in_specs=[vmem, vmem],
        out_specs=(anywhere, vmem),
        scratch_shapes=[dma((species,))],
        compiler_params=pltpu.CompilerParams(vmem_limit_bytes=8 << 20),
        name="finish",
    )(adv, sums)


def solution(mesh):
    in_specs = (
        P(None, "gx", "gy", "sec"),
        P("gx", "gy", "sec"),
        P("gx", "gy", "sec"),
        P(),
        P(),
        P("gx", "gy", "sec"),
        P(),
    )
    out_specs = (P(None, "gx", "gy", "sec"), P(None, "gx", None))
    return jax.shard_map(
        on_device, mesh=mesh, in_specs=in_specs, out_specs=out_specs, check_vma=False
    )
```

time: 39 us -> 33 us (0.85)
  the two profiles are of different devices: /device:TPU:16 before, /device:TPU:1 now
where the time goes in v2:
time: 33 us; the launch traced here: 32.9 us
  Pallas kernels  32.2 us (98%)
  between operations  0.64 us (2%)
    pallas_call x1, Pallas kernels, on_device(): pl.pallas_call(functools.partial(kernel, species), out_shape=(pltpu.VMEM(...  30.3 us
    pallas_call x1, Pallas kernels, on_device(): pl.pallas_call(finish, out_shape=(jax.ShapeDtypeStruct(comp.shape, F32),...  1.89 us

profile of v2, /device:TPU:1, one launch (start us, length us, event | category | flops | bytes accessed | tf_op | source)
XLA Modules:
  0.0 32.9 jit_solution(4084419153743807588)
XLA Ops:
  0.6 30.3 %section.1 = (f32[8,16,24,128]{3,2,1,0:T(8,128)S(1)}, f32[24,256]{1,0:T(8,128)S(1)}) custom-call(f32[22,8,16,128]{3,2,1,0:T(8,128)} %comp_hbm.1, f32[8,16,128]{2,1,0:T(8,128)} %diff_hbm.1, f32[8,16,128]{2,1,0:T(8,128)} %temp_hbm.1, f32[22]{0:T(128)} %weight_hbm.1, f32[22,22]{1,0:T(8,128)} %jac_hbm.1, s32[8,16,128]{2,1,0:T(8,128)} %bins_hbm.1, s32[128]{0:T(128)} %pos_hbm.1), custom_call_target="tpu_custom_call" | custom-call | tf_op jit(solution)/shard_map/section/pallas_call | solution.py:415
  31.0 1.9 %finish.1 = (f32[22,8,16,128]{3,2,1,0:T(8,128)}, f32[22,4,64]{2,1,0:T(4,128)}) custom-call(f32[8,16,24,128]{3,2,1,0:T(8,128)S(1)} %get-tuple-element.4.adv, f32[24,256]{1,0:T(8,128)S(1)} %get-tuple-element.5.sums), custom_call_target="tpu_custom_call" | custom-call | tf_op jit(solution)/shard_map/finish/pallas_call | solution.py:462

commit v3 on v2

--- a/solution.py
+++ b/solution.py
@@ -49,6 +49,11 @@
     onehot_z,
     rate,
     flux_x,
+    flux_z,
+    source_a,
+    source_b,
+    parts_a,
+    parts_b,
     temp,
     bins,
     jac,
@@ -106,12 +111,9 @@
         pltpu.make_async_copy(weight_hbm, weight, in_sem.at[27]),
         pltpu.make_async_copy(pos_hbm, pos, in_sem.at[28]),
     ]
-    for copy in loads:
-        copy.start()
-
     barrier = pltpu.get_barrier_semaphore()
+    inner_left, inner_right = gx > 0, gx < ngx - 1
     peers = [
-        device(sec, right, gy),
         device(sec, left, gy),
         device(sec, gx, front),
         device(sec, gx, back),
@@ -122,9 +124,16 @@
         at_xy(gx, my_x, lax.rem(my_y + 1, ny)),
         at_xy(gx, my_x, lax.rem(my_y + ny - 1, ny)),
     ]
+
+    @pl.when(inner_right)
+    def _():
+        pl.semaphore_signal(
+            barrier, inc=1, device_id=device(sec, right, gy), device_id_type=MESH
+        )
+
     for peer in peers:
         pl.semaphore_signal(barrier, inc=1, device_id=peer, device_id_type=MESH)
-    for copy in first:
+    for copy in first[0:2] + loads + first[2:]:
         copy.start()
 
     ones = jnp.ones((1, 128), F32)
@@ -156,40 +165,6 @@
     for s in range(species):
         wk = jnp.where(row_id == s, 0.025 * weight[s], wk)
 
-    for copy in loads:
-        copy.wait()
-    pl.semaphore_wait(barrier, len(peers))
-    halo = [
-        remote(u.at[8, 1:17], u.at[0, 1:17], hs_sem.at[0], hr_sem.at[0], device(sec, right, gy)),
-        remote(u.at[1, 1:17], u.at[9, 1:17], hs_sem.at[1], hr_sem.at[1], device(sec, left, gy)),
-        remote(u.at[1:9, 16], u.at[1:9, 0], hs_sem.at[2], hr_sem.at[2], device(sec, gx, front)),
-        remote(u.at[1:9, 1], u.at[1:9, 17], hs_sem.at[3], hr_sem.at[3], device(sec, gx, back)),
-        remote(zsend.at[1], zrecv.at[0], hs_sem.at[4], hr_sem.at[4], device(up, gx, gy)),
-        remote(zsend.at[0], zrecv.at[1], hs_sem.at[5], hr_sem.at[5], device(down, gx, gy)),
-    ]
-    for copy in halo[0:4]:
-        copy.start()
-
-    def pack(x, carry):
-        low, high = carry
-        heads = tails = None
-        for y in range(rows):
-            c = u[x + 1, y + 1]
-            turned = pltpu.roll(c, y, 1) if y else c
-            heads = turned if y == 0 else jnp.where(lane_id == y, turned, heads)
-            tails = turned if y == 0 else jnp.where(lane_id == y - 1, turned, tails)
-        here = lane_id // rows == x
-        low = jnp.where(here, pltpu.roll(heads, x * rows, 1), low)
-        high = jnp.where(here, pltpu.roll(tails, x * rows + 1, 1), high)
-        return low, high
-
-    blank = jnp.zeros((ROWS, 128), F32)
-    low, high = lax.fori_loop(0, planes, pack, (blank, blank))
-    zsend[0] = low
-    zsend[1] = high
-    for copy in halo[4:6]:
-        copy.start()
-
     across = jnp.transpose(bins[...].reshape(planes * rows, 128).astype(F32))
     lane1 = lax.broadcasted_iota(jnp.int32, (1, 128), 1)
     group_of = (lane1 // rows + 1) // 2
@@ -200,21 +175,82 @@
             jnp.broadcast_to(code, (5 * NB, 128)) == code_level, 1.0, 0.0
         ).astype(BF16)
 
+    @pl.when(jnp.logical_not(inner_left))
+    def _():
+        u[0] = jnp.zeros(u.shape[1:], F32)
+
+    @pl.when(jnp.logical_not(inner_right))
+    def _():
+        u[planes + 1] = jnp.zeros(u.shape[1:], F32)
+
+    for copy in loads:
+        copy.wait()
+    pl.semaphore_wait(barrier, len(peers) + jnp.minimum(gx, 1))
+
+    halo = [
+        remote(u.at[8, 1:17], u.at[0, 1:17], hs_sem.at[0], hr_sem.at[0], device(sec, right, gy)),
+        remote(u.at[1, 1:17], u.at[9, 1:17], hs_sem.at[1], hr_sem.at[1], device(sec, left, gy)),
+        remote(u.at[1:9, 16], u.at[1:9, 0], hs_sem.at[2], hr_sem.at[2], device(sec, gx, front)),
+        remote(u.at[1:9, 1], u.at[1:9, 17], hs_sem.at[3], hr_sem.at[3], device(sec, gx, back)),
+        remote(zsend.at[1], zrecv.at[0], hs_sem.at[4], hr_sem.at[4], device(up, gx, gy)),
+        remote(zsend.at[0], zrecv.at[1], hs_sem.at[5], hr_sem.at[5], device(down, gx, gy)),
+    ]
+
+    @pl.when(inner_right)
+    def _():
+        halo[0].start()
+
+    @pl.when(inner_left)
+    def _():
+        halo[1].start()
+
+    for copy in halo[2:4]:
+        copy.start()
+
+    packed = []
+    for x in range(planes):
+        heads = tails = None
+        for y in range(rows):
+            c = u[x + 1, y + 1]
+            turned = pltpu.roll(c, y, 1) if y else c
+            heads = turned if y == 0 else jnp.where(lane_id == y, turned, heads)
+            tails = turned if y == 0 else jnp.where(lane_id == y - 1, turned, tails)
+        packed.append((heads, tails))
+    low = high = None
+    for x, (heads, tails) in enumerate(packed):
+        heads = pltpu.roll(heads, x * rows, 1) if x else heads
+        tails = pltpu.roll(tails, x * rows + 1, 1)
+        here = lane_id >= x * rows
+        low = heads if x == 0 else jnp.where(here, heads, low)
+        high = tails if x == 0 else jnp.where(here, tails, high)
+    zsend[0] = low
+    zsend[1] = high
+    for copy in halo[4:6]:
+        copy.start()
+
     inside = lax.broadcasted_iota(jnp.int32, (1, 128), 1) < 127
 
-    def inner(x, carry):
+    def react(x, source):
         parts = split(jnp.concatenate([u[x + 1, y + 1] for y in range(rows)], axis=1))
-        source = jnp.dot(
+        source[...] = jnp.dot(
             j_all, jnp.concatenate([parts, parts], axis=0), preferred_element_type=F32
         )
-        done = []
+
+    def advance(x, source, parts):
         xp = jnp.minimum(x + 2, 8)
+        for y in range(rows):
+            c = u[x + 1, y + 1]
+            d = u[x + 1, y + 1, dif : dif + 1, :]
+            turned = pltpu.roll(c, 127, 1)
+            gain = jnp.where(inside, d + turned[dif : dif + 1], 0.0)
+            out = gain * (turned - c)
+            flux_z[y] = out - pltpu.roll(out, 1, 1)
         flux_y = None
         for y in range(rows):
             c = u[x + 1, y + 1]
             d = u[x + 1, y + 1, dif : dif + 1, :]
             after = (d + u[xp, y + 1, dif : dif + 1, :]) * (u[xp, y + 1] - c)
-            flux = after - flux_x[y]
+            flux = flux_z[y] + (after - flux_x[y])
             flux_x[y] = after
             if y < rows - 1:
                 later = (d + u[x + 1, y + 2, dif : dif + 1, :]) * (u[x + 1, y + 2] - c)
@@ -222,21 +258,39 @@
                 flux_y = later
             else:
                 flux = flux - flux_y
-            turned = pltpu.roll(c, 127, 1)
-            gain = jnp.where(inside, d + pltpu.roll(d, 127, 1), 0.0)
-            out = gain * (turned - c)
-            flux = flux + (out - pltpu.roll(out, 1, 1))
-            part = source[:, y * 128 : (y + 1) * 128]
-            value = (c + rate[x, pl.ds(y, 1), :] * part) + wk * flux
+            here = slice(y * 128, (y + 1) * 128)
+            value = (c + rate[x, pl.ds(y, 1), :] * source[:, here]) + wk * flux
             adv[x, y] = value
-            done.append(value)
-        psum[x] = binned(jnp.concatenate(done, axis=1), onehot[x])
+            parts[:, here] = split(value)
+
+    def collect(x, parts):
+        both = lax.dot_general(
+            parts[...], onehot[x], (((1,), (1,)), ((), ())), preferred_element_type=F32
+        )
+        psum[x] = both[0:ROWS] + both[ROWS : 2 * ROWS]
+
+    react(0, source_a)
+
+    def inner(x, carry):
+        collect(jnp.maximum(x - 1, 0), parts_b)
+        advance(x, source_a, parts_b)
+        react(jnp.minimum(x + 1, planes - 1), source_a)
         return carry
 
     lax.fori_loop(0, planes, inner, 0)
-
-    for copy in halo:
+    collect(planes - 1, parts_b)
+
+    for copy in halo[2:]:
         copy.wait_recv()
+
+    @pl.when(inner_left)
+    def _():
+        halo[0].wait_recv()
+
+    @pl.when(inner_right)
+    def _():
+        halo[1].wait_recv()
+
     near = [at_xy(gx, lax.rem(my_x + o, nx), my_y) for o in range(1, nx)]
     near += [at_xy(gx, my_x, lax.rem(my_y + o, ny)) for o in range(1, ny)]
     for peer in near:
@@ -249,7 +303,7 @@
         return jnp.where(there, 1.0, 0.0)
 
     faces_x = []
-    for x, ghost, gate in ((0, 0, gate_of(gx > 0)), (7, 9, gate_of(gx < ngx - 1))):
+    for x, ghost, gate in ((0, 0, 1.0), (7, 9, 1.0)):
         terms = []
         for y in range(rows):
             term = face(
@@ -382,13 +436,22 @@
         if o:
             block = r2b.at[0, my_x]
             send(block, block, s2b.at[0, o], q2b.at[0, my_x], at_xy(gx, peer, my_y))
-    for copy in halo + waits:
+    for copy in halo[2:] + waits:
         copy.wait_send()
+
+    @pl.when(inner_right)
+    def _():
+        halo[0].wait_send()
+
+    @pl.when(inner_left)
+    def _():
+        halo[1].wait_send()
+
     sums[8:24] = gather(r2b, q2b, my_x, nx, 2)
     sums[0:8] = gather(r2a, q2a, my_y, ny, 2)
 
 
-def finish(adv, sums, adv_hbm, cond_ref, out_sem):
+def finish(adv, sums, adv_hbm, cond_hbm, cond, out_sem):
     species = adv_hbm.shape[0]
     outs = [
         pltpu.make_async_copy(adv.at[:, :, s, :], adv_hbm.at[s], out_sem.at[s])
@@ -399,9 +462,12 @@
     whole = sums[...]
     means = whole / jnp.maximum(whole[ROWS - 1 : ROWS], 1.0)
     for part in range(4):
-        cond_ref[:, part, :] = means[0:species, part * NB : (part + 1) * NB]
+        cond[:, part, :] = means[0:species, part * NB : (part + 1) * NB]
+    last = pltpu.make_async_copy(cond, cond_hbm, out_sem.at[species])
+    last.start()
     for copy in outs:
         copy.wait()
+    last.wait()
 
 
 def on_device(comp, diff, temp, weight, jac, bins, pos):
@@ -426,6 +492,11 @@
             pltpu.VMEM((2, 5 * NB, cells), BF16),
             pltpu.VMEM((planes, rows, cells), F32),
             pltpu.VMEM((rows, ROWS, cells), F32),
+            pltpu.VMEM((rows, ROWS, cells), F32),
+            pltpu.VMEM((ROWS, rows * cells), F32),
+            pltpu.VMEM((ROWS, rows * cells), F32),
+            pltpu.VMEM((2 * ROWS, rows * cells), BF16),
+            pltpu.VMEM((2 * ROWS, rows * cells), BF16),
             pltpu.VMEM((planes, rows, cells), F32),
             pltpu.VMEM((planes, rows, cells), jnp.int32),
             pltpu.VMEM(jac.shape, F32),
@@ -466,8 +537,8 @@
             jax.ShapeDtypeStruct((species, per, NB), F32),
         ),
         in_specs=[vmem, vmem],
-        out_specs=(anywhere, vmem),
-        scratch_shapes=[dma((species,))],
+        out_specs=(anywhere, anywhere),
+        scratch_shapes=[pltpu.VMEM((species, per, NB), F32), dma((species + 1,))],
         compiler_params=pltpu.CompilerParams(vmem_limit_bytes=8 << 20),
         name="finish",
     )(adv, sums)

time: 33 us -> 30.3 us (0.918)
  the two profiles are of different devices: /device:TPU:1 before, /device:TPU:2 now
where the time goes in v3:
time: 30.3 us; the launch traced here: 30.1 us
  Pallas kernels  29.4 us (97%)
  between operations  0.64 us (2%)
    pallas_call x1, Pallas kernels, on_device(): pl.pallas_call(functools.partial(kernel, species), out_shape=(pltpu.VMEM(...  28.1 us
    pallas_call x1, Pallas kernels, on_device(): pl.pallas_call(finish, out_shape=(jax.ShapeDtypeStruct(comp.shape, F32),...  1.29 us

profile of v3, /device:TPU:2, one launch (start us, length us, event | category | flops | bytes accessed | tf_op | source)
XLA Modules:
  0.0 30.1 jit_solution(12493902986511300619)
XLA Ops:
  0.6 28.1 %section.1 = (f32[8,16,24,128]{3,2,1,0:T(8,128)S(1)}, f32[24,256]{1,0:T(8,128)S(1)}) custom-call(f32[22,8,16,128]{3,2,1,0:T(8,128)} %comp_hbm.1, f32[8,16,128]{2,1,0:T(8,128)} %diff_hbm.1, f32[8,16,128]{2,1,0:T(8,128)} %temp_hbm.1, f32[22]{0:T(128)} %weight_hbm.1, f32[22,22]{1,0:T(8,128)} %jac_hbm.1, s32[8,16,128]{2,1,0:T(8,128)} %bins_hbm.1, s32[128]{0:T(128)} %pos_hbm.1), custom_call_target="tpu_custom_call" | custom-call | tf_op jit(solution)/shard_map/section/pallas_call | solution.py:481
  28.8 1.3 %finish.1 = (f32[22,8,16,128]{3,2,1,0:T(8,128)}, f32[22,4,64]{2,1,0:T(4,128)}) custom-call(f32[8,16,24,128]{3,2,1,0:T(8,128)S(1)} %get-tuple-element.4.adv, f32[24,256]{1,0:T(8,128)S(1)} %get-tuple-element.5.sums), custom_call_target="tpu_custom_call" | custom-call | tf_op jit(solution)/shard_map/finish/pallas_call | solution.py:533

commit v4 on v3

--- a/solution.py
+++ b/solution.py
@@ -133,47 +133,19 @@
 
     for peer in peers:
         pl.semaphore_signal(barrier, inc=1, device_id=peer, device_id_type=MESH)
-    for copy in first[0:2] + loads + first[2:]:
+    for copy in loads + first:
         copy.start()
 
     ones = jnp.ones((1, 128), F32)
-    level = lax.broadcasted_iota(jnp.int32, (NB, 128), 0)
-    for copy in first:
-        copy.wait()
-
-    def prepare(x, carry):
-        for y in range(rows):
-            row = bins[x, pl.ds(y, 1), :]
-            onehot[x, :, y * 128 : (y + 1) * 128] = jnp.where(
-                jnp.broadcast_to(row, (NB, 128)) == level, 1.0, 0.0
-            ).astype(BF16)
+
+    def count_row(x, carry):
+        for y in range(rows):
             u[x + 1, y + 1, dif + 1 : dif + 2, :] = ones
-        rate[x] = 0.2 * jnp.exp(-2.0 / temp[x])
         return carry
 
-    lax.fori_loop(0, planes, prepare, 0)
-    flux_x[...] = jnp.zeros_like(flux_x)
-    jac_pad[...] = jnp.zeros_like(jac_pad)
-    jac_pad[0:species, 0:species] = jac[...]
-    j_full = jac_pad[...]
-    j_hi = j_full.astype(BF16).astype(F32)
-    j_lo = j_full - j_hi
-    j_all = jnp.concatenate([j_hi, j_hi, j_lo, j_lo], axis=1).astype(BF16)
+    lax.fori_loop(0, planes, count_row, 0)
     row_id = lax.broadcasted_iota(jnp.int32, (ROWS, 128), 0)
     lane_id = lax.broadcasted_iota(jnp.int32, (ROWS, 128), 1)
-    wk = jnp.zeros((ROWS, 128), F32)
-    for s in range(species):
-        wk = jnp.where(row_id == s, 0.025 * weight[s], wk)
-
-    across = jnp.transpose(bins[...].reshape(planes * rows, 128).astype(F32))
-    lane1 = lax.broadcasted_iota(jnp.int32, (1, 128), 1)
-    group_of = (lane1 // rows + 1) // 2
-    code_level = lax.broadcasted_iota(jnp.int32, (5 * NB, 128), 0)
-    for side, lane in ((0, 0), (1, 127)):
-        code = across[lane : lane + 1, :].astype(jnp.int32) + group_of * NB
-        onehot_z[side] = jnp.where(
-            jnp.broadcast_to(code, (5 * NB, 128)) == code_level, 1.0, 0.0
-        ).astype(BF16)
 
     @pl.when(jnp.logical_not(inner_left))
     def _():
@@ -227,6 +199,41 @@
     zsend[1] = high
     for copy in halo[4:6]:
         copy.start()
+
+    level = lax.broadcasted_iota(jnp.int32, (NB, 128), 0)
+    for copy in first:
+        copy.wait()
+
+    def prepare(x, carry):
+        for y in range(rows):
+            row = bins[x, pl.ds(y, 1), :]
+            onehot[x, :, y * 128 : (y + 1) * 128] = jnp.where(
+                jnp.broadcast_to(row, (NB, 128)) == level, 1.0, 0.0
+            ).astype(BF16)
+        rate[x] = 0.2 * jnp.exp(-2.0 / temp[x])
+        return carry
+
+    lax.fori_loop(0, planes, prepare, 0)
+    flux_x[...] = jnp.zeros_like(flux_x)
+    jac_pad[...] = jnp.zeros_like(jac_pad)
+    jac_pad[0:species, 0:species] = jac[...]
+    j_full = jac_pad[...]
+    j_hi = j_full.astype(BF16).astype(F32)
+    j_lo = j_full - j_hi
+    j_all = jnp.concatenate([j_hi, j_hi, j_lo, j_lo], axis=1).astype(BF16)
+    wk = jnp.zeros((ROWS, 128), F32)
+    for s in range(species):
+        wk = jnp.where(row_id == s, 0.025 * weight[s], wk)
+
+    across = jnp.transpose(bins[...].reshape(planes * rows, 128).astype(F32))
+    lane1 = lax.broadcasted_iota(jnp.int32, (1, 128), 1)
+    group_of = (lane1 // rows + 1) // 2
+    code_level = lax.broadcasted_iota(jnp.int32, (5 * NB, 128), 0)
+    for side, lane in ((0, 0), (1, 127)):
+        code = across[lane : lane + 1, :].astype(jnp.int32) + group_of * NB
+        onehot_z[side] = jnp.where(
+            jnp.broadcast_to(code, (5 * NB, 128)) == code_level, 1.0, 0.0
+        ).astype(BF16)
 
     inside = lax.broadcasted_iota(jnp.int32, (1, 128), 1) < 127
 

time: 30.3 us -> 31 us (1.023)
  the two profiles are of different devices: /device:TPU:2 before, /device:TPU:8 now
where the time goes in v4:
time: 31 us; the launch traced here: 30.8 us
  Pallas kernels  30.2 us (97%)
  between operations  0.64 us (2%)
    pallas_call x1, Pallas kernels, on_device(): pl.pallas_call(functools.partial(kernel, species), out_shape=(pltpu.VMEM(...  28.9 us
    pallas_call x1, Pallas kernels, on_device(): pl.pallas_call(finish, out_shape=(jax.ShapeDtypeStruct(comp.shape, F32),...  1.29 us

profile of v4, /device:TPU:8, one launch (start us, length us, event | category | flops | bytes accessed | tf_op | source)
XLA Modules:
  0.0 30.8 jit_solution(8816211659370577376)
XLA Ops:
  0.6 28.9 %section.1 = (f32[8,16,24,128]{3,2,1,0:T(8,128)S(1)}, f32[24,256]{1,0:T(8,128)S(1)}) custom-call(f32[22,8,16,128]{3,2,1,0:T(8,128)} %comp_hbm.1, f32[8,16,128]{2,1,0:T(8,128)} %diff_hbm.1, f32[8,16,128]{2,1,0:T(8,128)} %temp_hbm.1, f32[22]{0:T(128)} %weight_hbm.1, f32[22,22]{1,0:T(8,128)} %jac_hbm.1, s32[8,16,128]{2,1,0:T(8,128)} %bins_hbm.1, s32[128]{0:T(128)} %pos_hbm.1), custom_call_target="tpu_custom_call" | custom-call | tf_op jit(solution)/shard_map/section/pallas_call | solution.py:488
  29.6 1.3 %finish.1 = (f32[22,8,16,128]{3,2,1,0:T(8,128)}, f32[22,4,64]{2,1,0:T(4,128)}) custom-call(f32[8,16,24,128]{3,2,1,0:T(8,128)S(1)} %get-tuple-element.4.adv, f32[24,256]{1,0:T(8,128)S(1)} %get-tuple-element.5.sums), custom_call_target="tpu_custom_call" | custom-call | tf_op jit(solution)/shard_map/finish/pallas_call | solution.py:540

commit v5 on v3

--- a/solution.py
+++ b/solution.py
@@ -119,11 +119,11 @@
         device(sec, gx, back),
         device(up, gx, gy),
         device(down, gx, gy),
-        at_xy(gx, lax.rem(my_x + 1, nx), my_y),
-        at_xy(gx, lax.rem(my_x + nx - 1, nx), my_y),
         at_xy(gx, my_x, lax.rem(my_y + 1, ny)),
         at_xy(gx, my_x, lax.rem(my_y + ny - 1, ny)),
     ]
+    along_x = [at_xy(gx, lax.rem(my_x + o, nx), my_y) for o in range(1, nx)]
+    peers += along_x
 
     @pl.when(inner_right)
     def _():
@@ -206,6 +206,8 @@
 
     for copy in halo[2:4]:
         copy.start()
+    for peer in along_x:
+        pl.semaphore_signal(ready, inc=1, device_id=peer, device_id_type=MESH)
 
     packed = []
     for x in range(planes):
@@ -291,11 +293,6 @@
     def _():
         halo[1].wait_recv()
 
-    near = [at_xy(gx, lax.rem(my_x + o, nx), my_y) for o in range(1, nx)]
-    near += [at_xy(gx, my_x, lax.rem(my_y + o, ny)) for o in range(1, ny)]
-    for peer in near:
-        pl.semaphore_signal(ready, inc=1, device_id=peer, device_id_type=MESH)
-
     def face(c, d, other, d_other, gate):
         return wk * ((d + d_other * gate) * (other * gate - c))
 
@@ -349,10 +346,28 @@
             total = total + plane_sums[x]
         totals.append(total)
     totals.append(jnp.zeros_like(totals[0]))
-    for k in range(3):
-        pair = jnp.concatenate(totals[2 * k : 2 * k + 2], axis=1)
-        r1b[0, my_y, :, k * 128 : (k + 1) * 128] = pair[8:24]
-        r1a[0, my_x, :, k * 128 : (k + 1) * 128] = pair[0:8]
+    count = pos.shape[0] // 2
+    per = count // ngx
+    m = lax.rem(pos[gx * planes] - gx * per + count, count)
+
+    def stations(total):
+        p = [total[:, k * 128 : (k + 1) * 128] for k in range(3)]
+        turned = [pltpu.roll(v, NB, 1) for v in p]
+        high = lax.broadcasted_iota(jnp.int32, p[0].shape, 1) >= NB
+        q = [jnp.where(high, turned[k], turned[k - 1] if k else 0.0) for k in range(3)]
+        flag = [jnp.where(m == k, 1.0, 0.0) for k in range(4)]
+        zero = jnp.zeros_like(p[0])
+        shifted = (p + [zero], q + [zero], [zero] + p, [zero] + q)
+        out = []
+        for k in range(4):
+            out.append(sum(flag[i] * shifted[i][k] for i in range(4)))
+        return jnp.concatenate(out[0:2], axis=1), jnp.concatenate(out[2:4], axis=1)
+
+    grouped = jnp.concatenate(totals, axis=1)
+    own, following = stations(grouped[8:24])
+    r1b[0, my_y] = grouped[0:8]
+    r1a[0, my_x] = own
+    next_a[...] = following
 
     waits = []
 
@@ -363,12 +378,25 @@
 
     far_y = sorted(range(1, ny), key=lambda o: -min(o, ny - o))
     far_x = sorted(range(1, nx), key=lambda o: -min(o, nx - o))
-    for o in far_y:
-        block = r1b.at[0, my_y]
-        send(block, block, s1b.at[0, o], q1b.at[0, my_y], at_xy(gx, my_x, lax.rem(my_y + o, ny)))
-    for o in far_x:
-        block = r1a.at[0, my_x]
-        send(block, block, s1a.at[0, o], q1a.at[0, my_x], at_xy(gx, lax.rem(my_x + o, nx), my_y))
+
+    def along_y(block, send_sem, recv_sem):
+        for o in far_y:
+            peer = at_xy(gx, my_x, lax.rem(my_y + o, ny))
+            send(block, block, send_sem.at[0, o], recv_sem.at[0, my_y], peer)
+
+    def over_x(buffer, following, send_sem, recv_sem):
+        block = buffer.at[0, my_x]
+        for o in far_x + [0]:
+            x = lax.rem(my_x + o, nx)
+            peer = at_xy(right, x, my_y)
+            send(following, buffer.at[1, my_x], send_sem.at[1, o], recv_sem.at[1, my_x], peer)
+            if o:
+                peer = at_xy(gx, x, my_y)
+                send(block, block, send_sem.at[0, o], recv_sem.at[0, my_x], peer)
+
+    along_y(r1b.at[0, my_y], s1b, q1b)
+    pl.semaphore_wait(ready, len(along_x))
+    over_x(r1a, next_a, s1a, q1a)
 
     def ends_in(x, carry):
         a, b = carry
@@ -400,42 +428,12 @@
                     total = total + buffer[layer, slot]
         return total
 
-    count = pos.shape[0] // 2
-    per = count // ngx
-    m = lax.rem(pos[gx * planes] - gx * per + count, count)
-
-    def stations(total):
-        p = [total[:, k * 128 : (k + 1) * 128] for k in range(3)]
-        turned = [pltpu.roll(v, NB, 1) for v in p]
-        high = lax.broadcasted_iota(jnp.int32, p[0].shape, 1) >= NB
-        q = [jnp.where(high, turned[k], turned[k - 1] if k else 0.0) for k in range(3)]
-        flag = [jnp.where(m == k, 1.0, 0.0) for k in range(4)]
-        zero = jnp.zeros_like(p[0])
-        shifted = (p + [zero], q + [zero], [zero] + p, [zero] + q)
-        out = []
-        for k in range(4):
-            out.append(sum(flag[i] * shifted[i][k] for i in range(4)))
-        return jnp.concatenate(out[0:2], axis=1), jnp.concatenate(out[2:4], axis=1)
-
-    own, following = stations(gather(r1a, q1a, my_x, nx, 1))
-    r2a[0, my_y] = own
-    next_a[...] = following
-    pl.semaphore_wait(ready, len(near))
-    for o in far_y + [0]:
-        peer = lax.rem(my_y + o, ny)
-        send(next_a, r2a.at[1, my_y], s2a.at[1, o], q2a.at[1, my_y], at_xy(right, my_x, peer))
-        if o:
-            block = r2a.at[0, my_y]
-            send(block, block, s2a.at[0, o], q2a.at[0, my_y], at_xy(gx, my_x, peer))
+    r2a[0, my_y] = gather(r1a, q1a, my_x, nx, 2)
+    along_y(r2a.at[0, my_y], s2a, q2a)
     own, following = stations(gather(r1b, q1b, my_y, ny, 1))
     r2b[0, my_x] = own
     next_b[...] = following
-    for o in far_x + [0]:
-        peer = lax.rem(my_x + o, nx)
-        send(next_b, r2b.at[1, my_x], s2b.at[1, o], q2b.at[1, my_x], at_xy(right, peer, my_y))
-        if o:
-            block = r2b.at[0, my_x]
-            send(block, block, s2b.at[0, o], q2b.at[0, my_x], at_xy(gx, peer, my_y))
+    over_x(r2b, next_b, s2b, q2b)
     for copy in halo[2:] + waits:
         copy.wait_send()
 
@@ -447,8 +445,8 @@
     def _():
         halo[1].wait_send()
 
-    sums[8:24] = gather(r2b, q2b, my_x, nx, 2)
-    sums[0:8] = gather(r2a, q2a, my_y, ny, 2)
+    sums[0:8] = gather(r2b, q2b, my_x, nx, 2)
+    sums[8:24] = gather(r2a, q2a, my_y, ny, 1)
 
 
 def finish(adv, sums, adv_hbm, cond_hbm, cond, out_sem):
@@ -506,21 +504,21 @@
             pltpu.VMEM((planes, ROWS, NB), F32),
             pltpu.VMEM((2, ROWS, cells), F32),
             pltpu.VMEM((2, ROWS, cells), F32),
-            pltpu.VMEM((1, nx, 8, 6 * NB), F32),
-            pltpu.VMEM((1, ny, 16, 6 * NB), F32),
+            pltpu.VMEM((2, nx, 16, 4 * NB), F32),
+            pltpu.VMEM((1, ny, 8, 6 * NB), F32),
+            pltpu.VMEM((16, 4 * NB), F32),
             pltpu.VMEM((8, 4 * NB), F32),
-            pltpu.VMEM((16, 4 * NB), F32),
-            pltpu.VMEM((2, ny, 8, 4 * NB), F32),
-            pltpu.VMEM((2, nx, 16, 4 * NB), F32),
+            pltpu.VMEM((1, ny, 16, 4 * NB), F32),
+            pltpu.VMEM((2, nx, 8, 4 * NB), F32),
             dma((29,)),
             dma((6,)),
             dma((6,)),
-            dma((1, nx)),
-            dma((1, nx)),
+            dma((2, nx)),
+            dma((2, nx)),
             dma((1, ny)),
             dma((1, ny)),
-            dma((2, ny)),
-            dma((2, ny)),
+            dma((1, ny)),
+            dma((1, ny)),
             dma((2, nx)),
             dma((2, nx)),
             pltpu.SemaphoreType.REGULAR,

time: 30.3 us -> 30 us (0.990)
  the two profiles are of different devices: /device:TPU:2 before, /device:TPU:1 now
where the time goes in v5:
time: 30 us; the launch traced here: 29.4 us
  Pallas kernels  28.8 us (96%)
  between operations  0.64 us (2%)
    pallas_call x1, Pallas kernels, on_device(): pl.pallas_call(functools.partial(kernel, species), out_shape=(pltpu.VMEM(...  27.5 us
    pallas_call x1, Pallas kernels, on_device(): pl.pallas_call(finish, out_shape=(jax.ShapeDtypeStruct(comp.shape, F32),...  1.29 us

profile of v5, /device:TPU:1, one launch (start us, length us, event | category | flops | bytes accessed | tf_op | source)
XLA Modules:
  0.0 29.4 jit_solution(531309832552805054)
XLA Ops:
  0.6 27.5 %section.1 = (f32[8,16,24,128]{3,2,1,0:T(8,128)S(1)}, f32[24,256]{1,0:T(8,128)S(1)}) custom-call(f32[22,8,16,128]{3,2,1,0:T(8,128)} %comp_hbm.1, f32[8,16,128]{2,1,0:T(8,128)} %diff_hbm.1, f32[8,16,128]{2,1,0:T(8,128)} %temp_hbm.1, f32[22]{0:T(128)} %weight_hbm.1, f32[22,22]{1,0:T(8,128)} %jac_hbm.1, s32[8,16,128]{2,1,0:T(8,128)} %bins_hbm.1, s32[128]{0:T(128)} %pos_hbm.1), custom_call_target="tpu_custom_call" | custom-call | tf_op jit(solution)/shard_map/section/pallas_call | solution.py:479
  28.1 1.3 %finish.1 = (f32[22,8,16,128]{3,2,1,0:T(8,128)}, f32[22,4,64]{2,1,0:T(4,128)}) custom-call(f32[8,16,24,128]{3,2,1,0:T(8,128)S(1)} %get-tuple-element.4.adv, f32[24,256]{1,0:T(8,128)S(1)} %get-tuple-element.5.sums), custom_call_target="tpu_custom_call" | custom-call | tf_op jit(solution)/shard_map/finish/pallas_call | solution.py:531

commit v6 on v5

--- a/solution.py
+++ b/solution.py
@@ -282,16 +282,8 @@
     lax.fori_loop(0, planes, inner, 0)
     collect(planes - 1, parts_b)
 
-    for copy in halo[2:]:
+    for copy in halo[4:6]:
         copy.wait_recv()
-
-    @pl.when(inner_left)
-    def _():
-        halo[0].wait_recv()
-
-    @pl.when(inner_right)
-    def _():
-        halo[1].wait_recv()
 
     def face(c, d, other, d_other, gate):
         return wk * ((d + d_other * gate) * (other * gate - c))
@@ -299,21 +291,14 @@
     def gate_of(there):
         return jnp.where(there, 1.0, 0.0)
 
-    faces_x = []
-    for x, ghost, gate in ((0, 0, 1.0), (7, 9, 1.0)):
-        terms = []
-        for y in range(rows):
-            term = face(
-                u[x + 1, y + 1],
-                u[x + 1, y + 1, dif : dif + 1, :],
-                u[ghost, y + 1],
-                u[ghost, y + 1, dif : dif + 1, :],
-                gate,
-            )
-            adv[x, y] = adv[x, y] + term
-            terms.append(term)
-        faces_x.append(binned(jnp.concatenate(terms, axis=1), onehot[x]))
-
+    ends = []
+    for side, gate in ((0, gate_of(sec > 0)), (1, gate_of(sec < nsec - 1))):
+        c, other = zsend[side], zrecv[side]
+        ends.append(face(c, c[dif : dif + 1], other, other[dif : dif + 1], gate))
+    by_group = binned(ends[0], onehot_z[0]) + binned(ends[1], onehot_z[1])
+
+    for copy in halo[2:4]:
+        copy.wait_recv()
     gate_back, gate_front = gate_of(gy > 0), gate_of(gy < ngy - 1)
     plane_sums = []
     for x in range(planes):
@@ -330,15 +315,32 @@
             terms.append(term)
         hot = jnp.concatenate([onehot[x, :, 0:128], onehot[x, :, 15 * 128 : 16 * 128]], axis=1)
         total = psum[x] + binned(jnp.concatenate(terms, axis=1), hot)
-        if x in (0, 7):
-            total = total + faces_x[x // 7]
         plane_sums.append(total)
-    ends = []
-    for side, gate in ((0, gate_of(sec > 0)), (1, gate_of(sec < nsec - 1))):
-        c, other = zsend[side], zrecv[side]
-        ends.append(face(c, c[dif : dif + 1], other, other[dif : dif + 1], gate))
-    by_group = binned(ends[0], onehot_z[0]) + binned(ends[1], onehot_z[1])
-
+
+    @pl.when(inner_left)
+    def _():
+        halo[0].wait_recv()
+
+    @pl.when(inner_right)
+    def _():
+        halo[1].wait_recv()
+
+    faces_x = []
+    for x, ghost, gate in ((0, 0, 1.0), (7, 9, 1.0)):
+        terms = []
+        for y in range(rows):
+            term = face(
+                u[x + 1, y + 1],
+                u[x + 1, y + 1, dif : dif + 1, :],
+                u[ghost, y + 1],
+                u[ghost, y + 1, dif : dif + 1, :],
+                gate,
+            )
+            adv[x, y] = adv[x, y] + term
+            terms.append(term)
+        faces_x.append(binned(jnp.concatenate(terms, axis=1), onehot[x]))
+    plane_sums[0] = plane_sums[0] + faces_x[0]
+    plane_sums[7] = plane_sums[7] + faces_x[1]
     totals = []
     for g, members in enumerate(GROUPS):
         total = by_group[:, g * NB : (g + 1) * NB]
@@ -394,9 +396,9 @@
                 peer = at_xy(gx, x, my_y)
                 send(block, block, send_sem.at[0, o], recv_sem.at[0, my_x], peer)
 
-    along_y(r1b.at[0, my_y], s1b, q1b)
     pl.semaphore_wait(ready, len(along_x))
     over_x(r1a, next_a, s1a, q1a)
+    along_y(r1b.at[0, my_y], s1b, q1b)
 
     def ends_in(x, carry):
         a, b = carry

time: 30 us -> 30.1 us (level)
  no operation moved by 1% of the time
where the time goes in v6:
time: 30.1 us; the launch traced here: 29.6 us
  Pallas kernels  29 us (96%)
  between operations  0.64 us (2%)
    pallas_call x1, Pallas kernels, on_device(): pl.pallas_call(functools.partial(kernel, species), out_shape=(pltpu.VMEM(...  27.7 us
    pallas_call x1, Pallas kernels, on_device(): pl.pallas_call(finish, out_shape=(jax.ShapeDtypeStruct(comp.shape, F32),...  1.29 us

profile of v6, /device:TPU:1, one launch (start us, length us, event | category | flops | bytes accessed | tf_op | source)
XLA Modules:
  0.0 29.6 jit_solution(13118837622538331947)
XLA Ops:
  0.6 27.7 %section.1 = (f32[8,16,24,128]{3,2,1,0:T(8,128)S(1)}, f32[24,256]{1,0:T(8,128)S(1)}) custom-call(f32[22,8,16,128]{3,2,1,0:T(8,128)} %comp_hbm.1, f32[8,16,128]{2,1,0:T(8,128)} %diff_hbm.1, f32[8,16,128]{2,1,0:T(8,128)} %temp_hbm.1, f32[22]{0:T(128)} %weight_hbm.1, f32[22,22]{1,0:T(8,128)} %jac_hbm.1, s32[8,16,128]{2,1,0:T(8,128)} %bins_hbm.1, s32[128]{0:T(128)} %pos_hbm.1), custom_call_target="tpu_custom_call" | custom-call | tf_op jit(solution)/shard_map/section/pallas_call | solution.py:481
  28.3 1.3 %finish.1 = (f32[22,8,16,128]{3,2,1,0:T(8,128)}, f32[22,4,64]{2,1,0:T(4,128)}) custom-call(f32[8,16,24,128]{3,2,1,0:T(8,128)S(1)} %get-tuple-element.4.adv, f32[24,256]{1,0:T(8,128)S(1)} %get-tuple-element.5.sums), custom_call_target="tpu_custom_call" | custom-call | tf_op jit(solution)/shard_map/finish/pallas_call | solution.py:533
